TPU v7x, 512 devices: a whole 4x8x8 slice. The times are simulated.
512 devices in a mesh: bulk: 64 (over x, z, core), span: 8 (over y).
Axes of the slice: x: 4, y: 8, z: 8, core: 2. Of those that a mesh axis runs over, the one named last changes fastest.
Arguments:
- snapshots: float32 [1048576, 128], P(('span', 'bulk'))
- jac_blocks: bfloat16 [8192, 4, 128, 128], P(('span', 'bulk'))
- jac_cols: int32 [8192, 4], P(('span', 'bulk')), may hold values from 0 to 8191, as said below
Outputs:
- modes: float32 [1048576, 128], P(('span', 'bulk'))
- factor: float32 [128, 128], replicated
- jac_modes: bfloat16 [1048576, 128], P(('span', 'bulk'))
- reduced: float32 [128, 128], replicated
Inputs may be any that keep to these rules, and one draw needn't show every extreme that they name: jac_cols[r, 0] = r. Every column block lies in the die region of r (aligned runs of 1024 block rows) and within 16 block rows of the shard of 16 block rows that holds r.
All inputs are finite; a program needn't handle non-finite values.
Results may differ from a plain program's by a relative error of at most 0.0029.
The roundings to bfloat16 on the way count: a program that leaves them out, or rounds other values in their place, can miss the bound.
Values may be sent and summed in bfloat16 or wider, within the bound.
A program may use at most 64 MiB of HBM per device.

v0:
```python
import jax
import jax.numpy as jnp
from jax import lax
from jax.sharding import PartitionSpec as P


def with_halo(array, sides, width):
    for axis, dim in sides:
        size, length = (lax.axis_size(axis), array.shape[dim])
        up = [(i, (i + 1) % size) for i in range(size - 1)]
        down = [(j, i) for i, j in up]
        last = lax.slice_in_dim(array, length - width, length, axis=dim)
        initial = lax.slice_in_dim(array, 0, width, axis=dim)
        before = lax.ppermute(last, axis, up)
        after = lax.ppermute(initial, axis, down)
        array = jnp.concatenate([before, array, after], axis=dim)
    return array


def total_gram(partial_value):
    return lax.psum(partial_value, ("bulk", "span"))


def cholesky_step(data, row_count):
    high = lax.Precision.HIGHEST
    width = data.shape[1]
    partial_value = lax.dot_general(
        data, data, (((0,), (0,)), ((), ())), precision=high, preferred_element_type=jnp.float32
    )
    gram = total_gram(partial_value) / row_count
    lower = jnp.linalg.cholesky(gram)
    inverse = lax.linalg.triangular_solve(
        lower, jnp.eye(width, dtype=jnp.float32), left_side=True, lower=True
    )
    result = jnp.dot(data, inverse.T, precision=high, preferred_element_type=jnp.float32)
    return (result, lower)


def shards(snapshots, jac_blocks, jac_cols):
    high = lax.Precision.HIGHEST
    local_rows, width = snapshots.shape
    block_rows = jac_cols.shape[0]
    blk = jac_blocks.shape[2]
    row_count = local_rows * lax.axis_size(("bulk", "span"))
    first, lower1 = cholesky_step(snapshots, row_count)
    modes, lower2 = cholesky_step(first, row_count)
    factor = jnp.dot(lower2.T, lower1.T, precision=high, preferred_element_type=jnp.float32)
    modes_b = modes.astype(jnp.bfloat16)
    shard_start = (
        lax.axis_index("span") * lax.axis_size("bulk") + lax.axis_index("bulk")
    ) * block_rows
    relative = jac_cols - shard_start
    extended = with_halo(modes_b, (("bulk", 0),), local_rows)
    ext_blocks = extended.reshape(3 * block_rows, blk, width)
    picked = jnp.take(ext_blocks, relative + block_rows, axis=0)
    product = jnp.einsum("rnij,rnjk->rik", jac_blocks, picked, preferred_element_type=jnp.float32)
    jac_modes = product.astype(jnp.bfloat16).reshape(local_rows, width)
    partial_value = lax.dot_general(
        modes,
        jac_modes.astype(jnp.float32),
        (((0,), (0,)), ((), ())),
        precision=high,
        preferred_element_type=jnp.float32,
    )
    reduced = lax.psum(partial_value, ("bulk", "span")) / row_count
    return (modes, factor, jac_modes, reduced)


def solution(mesh):
    return jax.shard_map(
        shards,
        mesh=mesh,
        in_specs=(
            P(("span", "bulk"), None),
            P(("span", "bulk"), None, None, None),
            P(("span", "bulk"), None),
        ),
        out_specs=(P(("span", "bulk"), None), P(), P(("span", "bulk"), None), P()),
        check_vma=False,
    )
```

profile of v0, /device:TPU:1, one launch (start us, length us, event | category | flops | bytes accessed | tf_op | source)
XLA Modules:
  0.0 870.4 jit_solution(4245679873390945482)
XLA Ops:
  7.2 4.1 fusion.29
  11.4 266.6 %all-reduce.4.cloned.1.call-done = f32[128,128]{0,1:T(8,128)} async-done(((f32[128,128]{0,1:T(8,128)}), f32[128,128]{0,1:T(8,128)}) %all-reduce.4.cloned.1.call-update) | async-done | bytes 65552 | tf_op jit(solution)/shard_map/psum | solution.py:21
  278.0 0.8 broadcast_multiply_fusion.2
  279.0 0.9 fusion.17
  279.8 11.7 %cholesky.44 = f32[128,128]{1,0:T(8,128)S(1)} custom-call(f32[128,128]{1,0:T(8,128)S(1)} %fusion.17), custom_call_target="Cholesky" | custom-call | tf_op jit(solution)/shard_map/jit(cholesky)/cholesky | solution.py:31
  291.6 0.6 compare_reduce_fusion.1
  292.2 0.6 select_bitcast_fusion.1
  292.8 9.8 %custom-call.6 = f32[1,128,128]{1,2,0:T(8,128)S(1)} custom-call(f32[1,128,128]{2,1,0:T(8,128)S(1)} %select_bitcast_fusion.1), custom_call_target="InvertDiagBlocksLowerTriangular" | custom-call | tf_op jit(solution)/shard_map/triangular_solve/custom-call.0 | solution.py:32
  302.6 0.3 fusion.12
  302.9 2.2 fusion.30
  305.1 1.6 fusion.31
  307.0 250.7 %all-reduce.6.cloned.1.call-done = f32[128,128]{0,1:T(8,128)} async-done(((f32[128,128]{0,1:T(8,128)}), f32[128,128]{0,1:T(8,128)}) %all-reduce.6.cloned.1.call-update) | async-done | bytes 65552 | tf_op jit(solution)/shard_map/psum | solution.py:21
  557.7 0.8 broadcast_multiply_fusion.1
  558.6 0.9 fusion.15
  559.5 11.7 %cholesky.55 = f32[128,128]{1,0:T(8,128)S(1)} custom-call(f32[128,128]{1,0:T(8,128)S(1)} %fusion.15), custom_call_target="Cholesky" | custom-call | tf_op jit(solution)/shard_map/jit(cholesky)/cholesky | solution.py:31
  571.2 0.7 compare_reduce_fusion
  572.0 0.7 select_bitcast_fusion
  572.7 9.8 %custom-call.7 = f32[1,128,128]{1,2,0:T(8,128)S(1)} custom-call(f32[1,128,128]{2,1,0:T(8,128)S(1)} %select_bitcast_fusion), custom_call_target="InvertDiagBlocksLowerTriangular" | custom-call | tf_op jit(solution)/shard_map/triangular_solve/custom-call.0 | solution.py:32
  582.5 0.3 fusion.10
  582.8 2.9 fusion.28
  585.7 1.9 collective-permute-start.1
  587.6 3.6 collective-permute-start
  591.6 4.8 collective-permute-done.1
  596.4 1.3 collective-permute-done
  597.7 2.3 pad_maximum_fusion
  600.0 3.6 gather_fusion
  603.6 2.5 fusion.6
  606.1 1.4 fusion.32
  607.5 2.2 fusion.19
  609.6 252.7 %all-reduce.8.cloned.1.call-done = f32[128,128]{0,1:T(8,128)} async-done(((f32[128,128]{0,1:T(8,128)}), f32[128,128]{0,1:T(8,128)}) %all-reduce.8.cloned.1.call-update) | async-done | bytes 65552 | tf_op jit(solution)/shard_map/psum | solution.py:65
  862.3 0.8 broadcast_multiply_fusion
  863.2 0.7 copy.22
  (23 shorter events, 0.9 us)
Async XLA Ops:
  7.2 596.4 %copy-start = (bf16[16,4,128,128]{3,2,1,0:T(8,128)(2,1)S(1)}, bf16[16,4,128,128]{3,2,1,0:T(8,128)(2,1)}, u32[]{:S(2)}) copy-start(bf16[16,4,128,128]{3,2,1,0:T(8,128)(2,1)} %param.7) | copy-start | bytes 6291460
  7.2 270.8 %all-reduce.4.cloned.1.call-start = ((), (), s32[]{:S(2)}) async-start(), calls=%async_computation | async-start | bytes 131072 | tf_op jit(solution)/shard_map/psum | solution.py:21
  11.4 546.3 %all-reduce.6.cloned.1.call-start = ((), (), s32[]{:S(2)}) async-start(), calls=%async_computation.1 | async-start | bytes 131072 | tf_op jit(solution)/shard_map/psum | solution.py:21
  306.8 284.5 %copy-start.3 = (s32[16,4]{0,1:T(4,128)S(1)}, s32[16,4]{0,1:T(4,128)}, u32[]{:S(2)}) copy-start(s32[16,4]{0,1:T(4,128)} %param.8) | copy-start | bytes 772
  306.8 555.5 %all-reduce.8.cloned.1.call-start = ((), (), s32[]{:S(2)}) async-start(), calls=%async_computation.2 | async-start | bytes 131072 | tf_op jit(solution)/shard_map/psum | solution.py:65
  585.7 10.7 %collective-permute-start.1 = (bf16[2048,128]{1,0:T(8,128)(2,1)}, bf16[2048,128]{1,0:T(8,128)(2,1)S(1)}, u32[]{:S(2)}, u32[]{:S(2)}) collective-permute-start(bf16[2048,128]{1,0:T(8,128)(2,1)} %get-tuple-element.16), channel_id=1, source_target_pairs={{8,0},{16,8},{24,16},{32,24},{40,32},{48,40},{56,48},{64,56},{72,6... | collective-permute-start | bytes 1572872 | tf_op jit(solution)/shard_map/ppermute | solution.py:15
  587.6 10.1 %collective-permute-start = (bf16[2048,128]{1,0:T(8,128)(2,1)}, bf16[2048,128]{1,0:T(8,128)(2,1)S(1)}, u32[]{:S(2)}, u32[]{:S(2)}) collective-permute-start(bf16[2048,128]{1,0:T(8,128)(2,1)} %get-tuple-element.16), channel_id=1, source_target_pairs={{0,8},{8,16},{16,24},{24,32},{32,40},{40,48},{48,56},{56,64},{64,7... | collective-permute-start | bytes 1572872 | tf_op jit(solution)/shard_map/ppermute | solution.py:14
  603.6 2.5 copy-start.1
  606.0 257.9 %copy-start.2 = (bf16[16,128,128]{1,2,0:T(8,128)(2,1)}, bf16[16,128,128]{1,2,0:T(8,128)(2,1)S(1)}, u32[]{:S(2)}) copy-start(bf16[16,128,128]{1,2,0:T(8,128)(2,1)S(1)} %fusion.6) | copy-start | bytes 1572868
Sparse Core Ops, SparseCore 0:
  13.6 264.4 all-reduce.3
  306.9 250.7 all-reduce.5
  607.6 254.6 all-reduce.7
where the time goes:
time: 871 us; the launch traced here: 870 us
  waiting for transfers between devices  776 us (89%)
  other arithmetic  52.3 us (6%)
  matrix products  17.5 us (2%)
  between operations  13.9 us (2%)
    psum x2, waiting for transfers between devices, total_gram(): return lax.psum(partial_value, ('bulk', 'span'))  517 us
    psum x1, waiting for transfers between devices, shards(): reduced = lax.psum(partial_value, ('bulk', 'span')) / row_count  253 us
    another operation x6, other arithmetic, cholesky_step(): lower = jnp.linalg.cholesky(gram)  24.9 us
    another operation x4, other arithmetic, cholesky_step(): lax.linalg.triangular_solve(lower, jnp.eye(width, dtype=jnp.float32), lef...  20.9 us
  transfers between devices with their start and end apart: 5, of which 5 were waited for; matrix products, arithmetic and copies ran while one was open for 0% of the time, Pallas kernels for 0%

commit v1 on v0

--- a/solution.py
+++ b/solution.py
@@ -62,7 +62,7 @@
         precision=high,
         preferred_element_type=jnp.float32,
     )
-    reduced = lax.psum(partial_value, ("bulk", "span")) / row_count
+    reduced = lax.psum(lax.psum(partial_value, "span"), "bulk") / row_count
     return (modes, factor, jac_modes, reduced)
 
 

time: 871 us -> 871 us (level)
    psum x1 -> x2, waiting for transfers between devices: 253 us -> 252 us  [shards(): reduced = lax.psum(lax.psum(partial_value, 'span'), 'bulk') / row_count]
  transfers between devices with their start and end apart: 5 -> 6, of which waited for: 5 -> 6; matrix products, arithmetic and copies ran while one was open for 0% -> 0% of each run, Pallas kernels for 0% -> 0%
where the time goes in v1:
time: 871 us; the launch traced here: 870 us
  waiting for transfers between devices  776 us (89%)
  other arithmetic  52.3 us (6%)
  matrix products  17.5 us (2%)
  between operations  13.9 us (2%)
    psum x2, waiting for transfers between devices, total_gram(): return lax.psum(partial_value, ('bulk', 'span'))  517 us
    psum x2, waiting for transfers between devices, shards(): reduced = lax.psum(lax.psum(partial_value, 'span'), 'bulk') / row_count  252 us
    another operation x6, other arithmetic, cholesky_step(): lower = jnp.linalg.cholesky(gram)  24.9 us
    another operation x4, other arithmetic, cholesky_step(): lax.linalg.triangular_solve(lower, jnp.eye(width, dtype=jnp.float32), lef...  20.9 us
  transfers between devices with their start and end apart: 6, of which 6 were waited for; matrix products, arithmetic and copies ran while one was open for 0% of the time, Pallas kernels for 0%

profile of v1, /device:TPU:1, one launch (start us, length us, event | category | flops | bytes accessed | tf_op | source)
XLA Modules:
  0.0 870.1 jit_solution(14553217681948604228)
XLA Ops:
  7.2 4.1 fusion.29
  11.4 266.6 %all-reduce.5.cloned.1.call-done = f32[128,128]{0,1:T(8,128)} async-done(((f32[128,128]{0,1:T(8,128)}), f32[128,128]{0,1:T(8,128)}) %all-reduce.5.cloned.1.call-update) | async-done | bytes 65552 | tf_op jit(solution)/shard_map/psum | solution.py:21
  278.0 0.8 broadcast_multiply_fusion.2
  279.0 0.9 fusion.17
  279.8 11.7 %cholesky.44 = f32[128,128]{1,0:T(8,128)S(1)} custom-call(f32[128,128]{1,0:T(8,128)S(1)} %fusion.17), custom_call_target="Cholesky" | custom-call | tf_op jit(solution)/shard_map/jit(cholesky)/cholesky | solution.py:31
  291.6 0.6 compare_reduce_fusion.1
  292.2 0.6 select_bitcast_fusion.1
  292.8 9.8 %custom-call.6 = f32[1,128,128]{1,2,0:T(8,128)S(1)} custom-call(f32[1,128,128]{2,1,0:T(8,128)S(1)} %select_bitcast_fusion.1), custom_call_target="InvertDiagBlocksLowerTriangular" | custom-call | tf_op jit(solution)/shard_map/triangular_solve/custom-call.0 | solution.py:32
  302.9 2.2 fusion.30
  305.1 1.6 fusion.31
  307.0 250.7 %all-reduce.7.cloned.1.call-done = f32[128,128]{0,1:T(8,128)} async-done(((f32[128,128]{0,1:T(8,128)}), f32[128,128]{0,1:T(8,128)}) %all-reduce.7.cloned.1.call-update) | async-done | bytes 65552 | tf_op jit(solution)/shard_map/psum | solution.py:21
  557.7 0.8 broadcast_multiply_fusion.1
  558.6 0.9 fusion.15
  559.5 11.7 %cholesky.55 = f32[128,128]{1,0:T(8,128)S(1)} custom-call(f32[128,128]{1,0:T(8,128)S(1)} %fusion.15), custom_call_target="Cholesky" | custom-call | tf_op jit(solution)/shard_map/jit(cholesky)/cholesky | solution.py:31
  571.2 0.7 compare_reduce_fusion
  572.0 0.7 select_bitcast_fusion
  572.7 9.8 %custom-call.7 = f32[1,128,128]{1,2,0:T(8,128)S(1)} custom-call(f32[1,128,128]{2,1,0:T(8,128)S(1)} %select_bitcast_fusion), custom_call_target="InvertDiagBlocksLowerTriangular" | custom-call | tf_op jit(solution)/shard_map/triangular_solve/custom-call.0 | solution.py:32
  582.5 0.3 fusion.10
  582.8 2.9 fusion.28
  585.7 1.9 collective-permute-start.1
  587.6 3.6 collective-permute-start
  591.6 4.8 collective-permute-done.1
  596.4 1.3 collective-permute-done
  597.7 2.3 pad_maximum_fusion
  600.0 3.6 gather_fusion
  603.6 2.5 fusion.6
  606.1 1.4 fusion.32
  607.5 67.3 %all-reduce.9.cloned.1.call-done = f32[128,128]{0,1:T(8,128)} async-done(((f32[128,128]{0,1:T(8,128)}), f32[128,128]{0,1:T(8,128)}) %all-reduce.9.cloned.1.call-update) | async-done | bytes 65552 | tf_op jit(solution)/shard_map/psum | solution.py:65
  674.8 2.2 fusion.19
  677.0 185.0 %all-reduce.11.cloned.1.call-done = f32[128,128]{0,1:T(8,128)} async-done(((f32[128,128]{0,1:T(8,128)}), f32[128,128]{0,1:T(8,128)}) %all-reduce.11.cloned.1.call-update) | async-done | bytes 65552 | tf_op jit(solution)/shard_map/psum | solution.py:65
  861.9 0.8 broadcast_multiply_fusion
  862.8 0.7 copy.22
  (26 shorter events, 1.2 us)
Async XLA Ops:
  7.2 596.4 %copy-start = (bf16[16,4,128,128]{3,2,1,0:T(8,128)(2,1)S(1)}, bf16[16,4,128,128]{3,2,1,0:T(8,128)(2,1)}, u32[]{:S(2)}) copy-start(bf16[16,4,128,128]{3,2,1,0:T(8,128)(2,1)} %param.7) | copy-start | bytes 6291460
  7.2 270.8 %all-reduce.5.cloned.1.call-start = ((), (), s32[]{:S(2)}) async-start(), calls=%async_computation | async-start | bytes 131072 | tf_op jit(solution)/shard_map/psum | solution.py:21
  11.4 546.3 %all-reduce.7.cloned.1.call-start = ((), (), s32[]{:S(2)}) async-start(), calls=%async_computation.1 | async-start | bytes 131072 | tf_op jit(solution)/shard_map/psum | solution.py:21
  306.8 284.5 %copy-start.3 = (s32[16,4]{0,1:T(4,128)S(1)}, s32[16,4]{0,1:T(4,128)}, u32[]{:S(2)}) copy-start(s32[16,4]{0,1:T(4,128)} %param.8) | copy-start | bytes 772
  306.8 368.0 %all-reduce.9.cloned.1.call-start = ((), (), s32[]{:S(2)}) async-start(), calls=%async_computation.2 | async-start | bytes 131072 | tf_op jit(solution)/shard_map/psum | solution.py:65
  585.7 10.7 %collective-permute-start.1 = (bf16[2048,128]{1,0:T(8,128)(2,1)}, bf16[2048,128]{1,0:T(8,128)(2,1)S(1)}, u32[]{:S(2)}, u32[]{:S(2)}) collective-permute-start(bf16[2048,128]{1,0:T(8,128)(2,1)} %get-tuple-element.16), channel_id=1, source_target_pairs={{8,0},{16,8},{24,16},{32,24},{40,32},{48,40},{56,48},{64,56},{72,6... | collective-permute-start | bytes 1572872 | tf_op jit(solution)/shard_map/ppermute | solution.py:15
  587.6 10.1 %collective-permute-start = (bf16[2048,128]{1,0:T(8,128)(2,1)}, bf16[2048,128]{1,0:T(8,128)(2,1)S(1)}, u32[]{:S(2)}, u32[]{:S(2)}) collective-permute-start(bf16[2048,128]{1,0:T(8,128)(2,1)} %get-tuple-element.16), channel_id=1, source_target_pairs={{0,8},{8,16},{16,24},{24,32},{32,40},{40,48},{48,56},{56,64},{64,7... | collective-permute-start | bytes 1572872 | tf_op jit(solution)/shard_map/ppermute | solution.py:14
  603.6 2.5 copy-start.1
  606.0 257.5 %copy-start.2 = (bf16[16,128,128]{1,2,0:T(8,128)(2,1)}, bf16[16,128,128]{1,2,0:T(8,128)(2,1)S(1)}, u32[]{:S(2)}) copy-start(bf16[16,128,128]{1,2,0:T(8,128)(2,1)S(1)} %fusion.6) | copy-start | bytes 1572868
  607.5 254.5 %all-reduce.11.cloned.1.call-start = ((), (), s32[]{:S(2)}) async-start(), calls=%async_computation.3 | async-start | bytes 131072 | tf_op jit(solution)/shard_map/psum | solution.py:65
Sparse Core Ops, SparseCore 0:
  13.6 264.4 all-reduce.4
  306.9 250.7 all-reduce.6
  607.6 67.1 all-reduce.8
  678.5 183.3 all-reduce.10
